TPU v7x, 512 devices: a whole 4x4x16 slice. The times are simulated.
512 devices in a mesh: seq: 64 (over y, z_lo, core), strand: 2 (over z_hi), head: 4 (over x).
Axes of the slice: x: 4, y: 4, z: 16 (z_hi: 2, z_lo: 8; z = z_hi * 8 + z_lo), core: 2. Of those that a mesh axis runs over, the one named last changes fastest.
Arguments:
- top: bfloat16 [4, 2, 16384, 1536], P('head', 'strand', 'seq'), may hold values from -6 to 6
- grad_heads: bfloat16 [4, 2, 16384, 1536], P(None, 'strand', 'seq', 'head'), may hold values from -6 to 6
- tap_weight_grid: bfloat16 [3, 768, 768], P(None, 'seq'), may hold values from -0.125 to 0.125
- out_w: bfloat16 [768, 768], P('seq'), may hold values from -0.21875 to 0.21875
- mix_w: bfloat16 [768, 768], P('seq'), may hold values from -0.21875 to 0.21875
- rc_perm: int32 [768], replicated, may hold values from 0 to 767, each once
Outputs:
- restored: bfloat16 [4, 2, 16384, 1536], P('head', 'strand', 'seq')
- grad_input: bfloat16 [4, 2, 16384, 1536], P('head', 'strand', 'seq')
Inputs may be any that keep to these rules, and one draw needn't show every extreme that they name: `rc_perm`: every channel index appears exactly once.
All inputs are finite; a program needn't handle non-finite values.
Results may differ from a plain program's by a relative error of at most 0.008.
Values may be sent and summed in bfloat16 or wider, within the bound.
No kernel may reach another device: no remote copies, remote signals or barrier semaphores. Data moves between devices by JAX's collectives and lax.ppermute only.
A program may use at most 64 MiB of HBM per device.

v0:
```python
import jax
import jax.numpy as jnp
from jax import lax
from jax.sharding import PartitionSpec as P


def rows_first(arrays, axis, dims):
    turned = [jnp.moveaxis(a, dim, 0) for a, dim in zip(arrays, dims)]
    widths = [t[0].size for t in turned]
    both = jnp.concatenate([t.reshape(-1, w) for t, w in zip(turned, widths)], axis=1)
    result = lax.all_gather(both, axis, axis=0, tiled=True)
    pieces = jnp.split(result, [sum(widths[:k]) for k in range(1, len(widths))], axis=1)
    return tuple(
        (
            jnp.moveaxis(b.reshape(-1, *t.shape[1:]), 0, dim)
            for b, t, dim in zip(pieces, turned, dims)
        )
    )


def swapped(value, axis, bit):
    mask = 2**bit
    pairs = [(source, source ^ mask) for source in range(lax.axis_size(axis))]
    return lax.ppermute(value, axis, pairs)


def with_halo(array, sides, width):
    for axis, dim in sides:
        devices, length = (lax.axis_size(axis), array.shape[dim])
        up = [(i, (i + 1) % devices) for i in range(devices - 1)]
        down = [(j, i) for i, j in up]
        last = lax.slice_in_dim(array, length - width, length, axis=dim)
        first = lax.slice_in_dim(array, 0, width, axis=dim)
        before = lax.ppermute(last, axis, up)
        after = lax.ppermute(first, axis, down)
        array = jnp.concatenate([before, array, after], axis=dim)
    return array


def taps_forward(padded, kernel, length, dilation):
    total = jnp.dot(padded[0:length], kernel[0], preferred_element_type=jnp.float32)
    total = total + jnp.dot(
        padded[dilation : dilation + length], kernel[1], preferred_element_type=jnp.float32
    )
    return total + jnp.dot(
        padded[2 * dilation : 2 * dilation + length], kernel[2], preferred_element_type=jnp.float32
    )


def taps_backward(padded, kernel, length, dilation):
    total = jnp.einsum(
        "pd,cd->pc",
        padded[2 * dilation : 2 * dilation + length],
        kernel[0],
        preferred_element_type=jnp.float32,
    )
    total = total + jnp.einsum(
        "pd,cd->pc",
        padded[dilation : dilation + length],
        kernel[1],
        preferred_element_type=jnp.float32,
    )
    return total + jnp.einsum(
        "pd,cd->pc", padded[0:length], kernel[2], preferred_element_type=jnp.float32
    )


def shards(top, grad_heads, tap_weight_grid, out_w, mix_w, rc_perm):
    length = top.shape[2]
    dilation = length // 2
    half = top.shape[3] // 2
    cotan = lax.all_to_all(grad_heads, "head", split_axis=0, concat_axis=3, tiled=True)[0, 0]
    conv_full, out_full, mix_full = rows_first((tap_weight_grid, out_w, mix_w), "seq", (1, 0, 0))
    top_a = top[0, 0, :, :half]
    top_b = top[0, 0, :, half:]
    grad_a = cotan[:, :half]
    second_gradient = cotan[:, half:]
    inverse = jnp.zeros((half,), jnp.int32).at[rc_perm].set(jnp.arange(half, dtype=jnp.int32))
    other_a = swapped(top_a, "strand", 0)
    mirror = jnp.take(other_a, rc_perm, axis=1)
    paired = (top_a.astype(jnp.float32) + mirror.astype(jnp.float32)).astype(jnp.bfloat16)
    mixing = jnp.dot(paired, mix_full, preferred_element_type=jnp.float32)
    second_input = (top_b.astype(jnp.float32) - mixing).astype(jnp.bfloat16)
    padded_b = with_halo(second_input, (("seq", 0),), dilation)
    preactivation_rows = taps_forward(padded_b, conv_full, length, dilation)
    hidden = jax.nn.gelu(preactivation_rows).astype(jnp.bfloat16)
    branch_out = jnp.dot(hidden, out_full, preferred_element_type=jnp.float32)
    input_a = (top_a.astype(jnp.float32) - branch_out).astype(jnp.bfloat16)
    backed = jnp.einsum(
        "pd,cd->pc", second_gradient, mix_full, preferred_element_type=jnp.float32
    ).astype(jnp.bfloat16)
    returned = swapped(jnp.take(backed, inverse, axis=1), "strand", 0)
    cot_a = (
        grad_a.astype(jnp.float32) + backed.astype(jnp.float32) + returned.astype(jnp.float32)
    ).astype(jnp.bfloat16)
    pulled = jnp.einsum("pd,cd->pc", cot_a, out_full, preferred_element_type=jnp.float32)
    unused, slope = jax.vjp(jax.nn.gelu, preactivation_rows)
    preactivation_cotangent = slope(pulled)[0].astype(jnp.bfloat16)
    padded_cot = with_halo(preactivation_cotangent, (("seq", 0),), dilation)
    cotangent_second = (
        second_gradient.astype(jnp.float32) + taps_backward(padded_cot, conv_full, length, dilation)
    ).astype(jnp.bfloat16)
    restored = jnp.concatenate([input_a, second_input], axis=1)[None, None]
    grad_input = jnp.concatenate([cot_a, cotangent_second], axis=1)[None, None]
    return (restored, grad_input)


def solution(mesh):
    placed = (
        P("head", "strand", "seq", None),
        P(None, "strand", "seq", "head"),
        P(None, "seq", None),
        P("seq", None),
        P("seq", None),
        P(),
    )
    return jax.shard_map(
        shards,
        mesh=mesh,
        in_specs=placed,
        out_specs=(P("head", "strand", "seq", None), P("head", "strand", "seq", None)),
        check_vma=False,
    )
```

profile of v0, /device:TPU:111, one launch (start us, length us, event | category | flops | bytes accessed | tf_op | source)
XLA Modules:
  0.0 258.7 jit_solution(8820897414289662014)
XLA Ops:
  8.2 1.4 maximum_bitcast_fusion.2
  10.7 12.7 %collective-permute-start = (bf16[256,768]{1,0:T(8,128)(2,1)S(1)}, bf16[256,768]{1,0:T(8,128)(2,1)S(1)}, u32[]{:S(2)}, u32[]{:S(2)}) collective-permute-start(bf16[256,768]{1,0:T(8,128)(2,1)S(1)} %slice_bitcast_fusion.9), channel_id=1, source_target_pairs={{0,4},{4,0},{1,5},{5,1},{2,6},{6,2},{3,7},{7,3},{8,12},{12,8},{9,1... | collective-permute-start | bytes 1179656 | tf_op jit(solution)/shard_map/ppermute | solution.py:24
  23.4 4.2 %all-to-all-start = ((bf16[4,1,256,384]{3,2,1,0:T(8,128)(2,1)}), bf16[4,1,256,384]{3,2,1,0:T(8,128)(2,1)S(1)}, u32[]{:S(2)}, u32[]{:S(2)}) async-start(bf16[4,1,256,384]{3,2,1,0:T(8,128)(2,1)} %param.9), calls=%async_computation | async-start | bytes 1572864 | tf_op jit(solution)/shard_map/all_to_all | solution.py:72
  27.7 3.4 %scatter_custom_fusion = s32[768]{0:T(1024)S(1)} fusion(s32[768]{0:T(1024)S(1)} %compare_select_fusion.1, s32[768]{0:T(1024)S(1)} %iota.3, s32[]{:T(128)} %constant.9.clone.1), kind=kCustom, calls=%fused_computation.68 | custom fusion | bytes 3076 | tf_op jit(solution)/shard_map/scatter | solution.py:78
  31.1 16.4 %collective-permute-done = bf16[256,768]{1,0:T(8,128)(2,1)S(1)} collective-permute-done((bf16[256,768]{1,0:T(8,128)(2,1)S(1)}, bf16[256,768]{1,0:T(8,128)(2,1)S(1)}, u32[]{:S(2)}, u32[]{:S(2)}) %collective-permute-start) | collective-permute-done | bytes 393248 | tf_op jit(solution)/shard_map/ppermute | solution.py:24
  47.7 2.7 %gather_fusion = bf16[768,256]{1,0:T(8,128)(2,1)S(1)} fusion(bf16[256,768]{0,1:T(8,128)(2,1)S(1)} %copy.27, s32[1024]{0:T(1024)S(1)} %pad_clamp_fusion.1), kind=kCustom, calls=%fused_computation.clone | custom fusion | bytes 789504 | tf_op jit(solution)/shard_map/jit(_take)/gather | solution.py:80
  51.3 1.2 copy.34
  52.4 111.7 %all-gather.3.cloned.1.call-done = bf16[64,12,3840]{2,1,0:T(8,128)(2,1)} async-done(((bf16[1,12,3840]{2,1,0:T(8,128)(2,1)}), bf16[64,12,3840]{2,1,0:T(8,128)(2,1)}) %all-gather.3.cloned.1.call-update) | async-done | bytes 5898256 | tf_op jit(solution)/shard_map/all_gather | solution.py:11
  164.1 9.6 %reshape.49 = bf16[768,3840]{1,0:T(8,128)(2,1)} reshape(bf16[64,12,3840]{2,1,0:T(8,128)(2,1)} %all-gather.3.cloned.1.call-done) | data formatting | bytes 11796480
  173.7 2.0 slice-done.2
  175.7 3.6 %copy.30 = bf16[768,2304]{0,1:T(8,128)(2,1)} copy(bf16[768,2304]{1,0:T(8,128)(2,1)S(1)} %slice-done.2) | data formatting | bytes 7077888 | tf_op jit(solution)/shard_map/split | solution.py:12
  179.3 2.2 fusion.3
  181.5 2.2 collective-permute-start.2
  183.7 4.6 %collective-permute-start.1 = (bf16[128,768]{1,0:T(8,128)(2,1)S(1)}, bf16[128,768]{1,0:T(8,128)(2,1)S(1)}, u32[]{:S(2)}, u32[]{:S(2)}) collective-permute-start(bf16[128,768]{1,0:T(8,128)(2,1)S(1)} %get-tuple-element.11), channel_id=1, source_target_pairs={{0,8},{8,16},{16,24},{24,32},{32,40},{40,48},{48,56},{56,64},{64,7... | collective-permute-start | bytes 589832 | tf_op jit(solution)/shard_map/ppermute | solution.py:34
  188.3 1.7 fusion.6
  190.0 2.7 %gather_fusion.1 = bf16[768,256]{1,0:T(8,128)(2,1)S(1)} fusion(bf16[256,768]{0,1:T(8,128)(2,1)S(1)} %fusion.6, s32[1024]{0:T(1024)S(1)} %pad_clamp_fusion), kind=kCustom, calls=%fused_computation.1.clone | custom fusion | bytes 789504 | tf_op jit(solution)/shard_map/jit(_take)/gather | solution.py:92
  192.9 2.5 collective-permute-start.3
  195.4 1.9 fusion.8
  197.3 1.8 fusion.10
  200.2 2.3 fusion.4
  203.4 32.8 %collective-permute-done.3 = bf16[256,768]{0,1:T(8,128)(2,1)S(1)} collective-permute-done((bf16[256,768]{0,1:T(8,128)(2,1)S(1)}, bf16[256,768]{0,1:T(8,128)(2,1)S(1)}, u32[]{:S(2)}, u32[]{:S(2)}) %collective-permute-start.3) | collective-permute-done | bytes 393248 | tf_op jit(solution)/shard_map/ppermute | solution.py:24
  237.2 4.6 %collective-permute-start.5 = (bf16[128,768]{1,0:T(8,128)(2,1)S(1)}, bf16[128,768]{1,0:T(8,128)(2,1)S(1)}, u32[]{:S(2)}, u32[]{:S(2)}) collective-permute-start(bf16[128,768]{1,0:T(8,128)(2,1)S(1)} %get-tuple-element.10), channel_id=1, source_target_pairs={{0,8},{8,16},{16,24},{24,32},{32,40},{40,48},{48,56},{56,64},{64,7... | collective-permute-start | bytes 589832 | tf_op jit(solution)/shard_map/ppermute | solution.py:34
  241.8 1.9 collective-permute-start.4
  245.0 5.0 %collective-permute-done.4 = bf16[128,768]{1,0:T(8,128)(2,1)S(1)} collective-permute-done((bf16[128,768]{1,0:T(8,128)(2,1)S(1)}, bf16[128,768]{1,0:T(8,128)(2,1)S(1)}, u32[]{:S(2)}, u32[]{:S(2)}) %collective-permute-start.4) | collective-permute-done | bytes 196640 | tf_op jit(solution)/shard_map/ppermute | solution.py:35
  (45 shorter events, 9.5 us)
Async XLA Ops:
  7.2 157.0 %all-gather.3.cloned.1.call-start = ((), (), s32[]{:S(2)}) async-start(), calls=%async_computation.1 | async-start | bytes 7987200 | tf_op jit(solution)/shard_map/all_gather | solution.py:11
  8.1 19.5 %copy-start.3 = (s32[768]{0:T(1024)S(1)}, s32[768]{0:T(1024)}, u32[]{:S(2)}) copy-start(s32[768]{0:T(1024)} %param.13) | copy-start | bytes 9220
  10.7 36.8 %collective-permute-start = (bf16[256,768]{1,0:T(8,128)(2,1)S(1)}, bf16[256,768]{1,0:T(8,128)(2,1)S(1)}, u32[]{:S(2)}, u32[]{:S(2)}) collective-permute-start(bf16[256,768]{1,0:T(8,128)(2,1)S(1)} %slice_bitcast_fusion.9), channel_id=1, source_target_pairs={{0,4},{4,0},{1,5},{5,1},{2,6},{6,2},{3,7},{7,3},{8,12},{12,8},{9,1... | collective-permute-start | bytes 1179656 | tf_op jit(solution)/shard_map/ppermute | solution.py:24
  23.4 27.8 %all-to-all-start = ((bf16[4,1,256,384]{3,2,1,0:T(8,128)(2,1)}), bf16[4,1,256,384]{3,2,1,0:T(8,128)(2,1)S(1)}, u32[]{:S(2)}, u32[]{:S(2)}) async-start(bf16[4,1,256,384]{3,2,1,0:T(8,128)(2,1)} %param.9), calls=%async_computation | async-start | bytes 1572864 | tf_op jit(solution)/shard_map/all_to_all | solution.py:72
  173.7 2.0 slice-start.2
  179.3 9.0 %copy-start.1 = (bf16[1,1,256,4,384]{2,4,3,1,0:T(8,128)(2,1)S(1)}, bf16[1,1,256,4,384]{2,4,3,1,0:T(8,128)(2,1)}, u32[]{:S(2)}) copy-start(bf16[1,1,256,4,384]{2,4,3,1,0:T(8,128)(2,1)} %copy.34) | copy-start | bytes 2359300
  181.5 15.8 %collective-permute-start.2 = (bf16[128,768]{1,0:T(8,128)(2,1)S(1)}, bf16[128,768]{1,0:T(8,128)(2,1)S(1)}, u32[]{:S(2)}, u32[]{:S(2)}) collective-permute-start(bf16[128,768]{1,0:T(8,128)(2,1)S(1)} %get-tuple-element.12), channel_id=1, source_target_pairs={{8,0},{16,8},{24,16},{32,24},{40,32},{48,40},{56,48},{64,56},{72,6... | collective-permute-start | bytes 589832 | tf_op jit(solution)/shard_map/ppermute | solution.py:35
  183.7 15.4 %collective-permute-start.1 = (bf16[128,768]{1,0:T(8,128)(2,1)S(1)}, bf16[128,768]{1,0:T(8,128)(2,1)S(1)}, u32[]{:S(2)}, u32[]{:S(2)}) collective-permute-start(bf16[128,768]{1,0:T(8,128)(2,1)S(1)} %get-tuple-element.11), channel_id=1, source_target_pairs={{0,8},{8,16},{16,24},{24,32},{32,40},{40,48},{48,56},{56,64},{64,7... | collective-permute-start | bytes 589832 | tf_op jit(solution)/shard_map/ppermute | solution.py:34
  192.9 43.3 %collective-permute-start.3 = (bf16[256,768]{0,1:T(8,128)(2,1)S(1)}, bf16[256,768]{0,1:T(8,128)(2,1)S(1)}, u32[]{:S(2)}, u32[]{:S(2)}) collective-permute-start(bf16[256,768]{0,1:T(8,128)(2,1)S(1)} %select_bitcast_fusion), channel_id=1, source_target_pairs={{0,4},{4,0},{1,5},{5,1},{2,6},{6,2},{3,7},{7,3},{8,12},{12,8},{9,1... | collective-permute-start | bytes 1179656 | tf_op jit(solution)/shard_map/ppermute | solution.py:24
  195.4 3.8 %copy-start = (bf16[768,2304]{0,1:T(8,128)(2,1)S(1)}, bf16[768,2304]{0,1:T(8,128)(2,1)}, u32[]{:S(2)}) copy-start(bf16[768,2304]{0,1:T(8,128)(2,1)} %copy.30) | copy-start | bytes 10616836
  199.1 1.1 copy-start.2
  199.1 37.2 %slice-start = ((s8[5898240]{0:T(1024)(128)(4,1)}), s8[4194304]{0:T(1024)(128)(4,1)S(1)}, s32[]{:S(2)}) async-start(s8[5898240]{0:T(1024)(128)(4,1)} %bitcast.63), calls=%async_computation.2 | async-start | bytes 8388608
  200.2 36.1 %slice-start.1 = ((s8[5898240]{0:T(1024)(128)(4,1)}), s8[1703936]{0:T(1024)(128)(4,1)S(1)}, s32[]{:S(2)}) async-start(s8[5898240]{0:T(1024)(128)(4,1)} %bitcast.63), calls=%async_computation.3 | async-start | bytes 3407872
  237.2 7.2 %collective-permute-start.5 = (bf16[128,768]{1,0:T(8,128)(2,1)S(1)}, bf16[128,768]{1,0:T(8,128)(2,1)S(1)}, u32[]{:S(2)}, u32[]{:S(2)}) collective-permute-start(bf16[128,768]{1,0:T(8,128)(2,1)S(1)} %get-tuple-element.10), channel_id=1, source_target_pairs={{0,8},{8,16},{16,24},{24,32},{32,40},{40,48},{48,56},{56,64},{64,7... | collective-permute-start | bytes 589832 | tf_op jit(solution)/shard_map/ppermute | solution.py:34
  241.8 8.2 %collective-permute-start.4 = (bf16[128,768]{1,0:T(8,128)(2,1)S(1)}, bf16[128,768]{1,0:T(8,128)(2,1)S(1)}, u32[]{:S(2)}, u32[]{:S(2)}) collective-permute-start(bf16[128,768]{1,0:T(8,128)(2,1)S(1)} %get-tuple-element.9), channel_id=1, source_target_pairs={{8,0},{16,8},{24,16},{32,24},{40,32},{48,40},{56,48},{64,56},{72,6... | collective-permute-start | bytes 589832 | tf_op jit(solution)/shard_map/ppermute | solution.py:35
Sparse Core Ops, SparseCore 0:
  10.1 153.9 all-gather.2
where the time goes:
time: 259 us
  waiting for transfers between devices  166 us (64%)
  starting transfers between devices  32.8 us (13%)
  local copies, waits for them, and re-layouts  29.9 us (12%)
  between operations  14.4 us (6%)
  matrix products  13 us (5%)
  other arithmetic  2.79 us (1%)
    all_gather x1, waiting for transfers between devices, rows_first(): result = lax.all_gather(both, axis, axis=0, tiled=True)  112 us
    ppermute x2, waiting for transfers between devices, swapped(): return lax.ppermute(value, axis, pairs)  49.1 us
    ppermute x2, starting transfers between devices, swapped(): return lax.ppermute(value, axis, pairs)  15.2 us
    unnamed x16, local copies, waits for them, and re-layouts  11.4 us
    ppermute x2, starting transfers between devices, with_halo(): before = lax.ppermute(last, axis, up)  9.16 us
    split x3, local copies, waits for them, and re-layouts, rows_first(): jnp.split(result, [sum(widths[:k]) for k in range(1, len(widths))], axis=1)  5.56 us
  transfers between devices with their start and end apart: 8, of which 5 were waited for; matrix products, arithmetic and copies ran while one was open for 9% of the time, Pallas kernels for 0%

commit v1 on v0

--- a/solution.py
+++ b/solution.py
@@ -8,7 +8,14 @@
     turned = [jnp.moveaxis(a, dim, 0) for a, dim in zip(arrays, dims)]
     widths = [t[0].size for t in turned]
     both = jnp.concatenate([t.reshape(-1, w) for t, w in zip(turned, widths)], axis=1)
-    result = lax.all_gather(both, axis, axis=0, tiled=True)
+
+    def track_series_all_up(frame_in):
+        finding = jnp.stack([frame_in for _ in range(lax.axis_size(axis))])
+        block_last = lax.all_to_all(finding, axis, concat_axis=0, split_axis=0)
+        d_next = jnp.concatenate(block_last, axis=0)
+        return d_next
+
+    result = track_series_all_up(both)
     pieces = jnp.split(result, [sum(widths[:k]) for k in range(1, len(widths))], axis=1)
     return tuple(
         (

time: 259 us -> 505 us (1.95)
  the two profiles are of different devices: /device:TPU:111 before, /device:TPU:1 now
where the time goes in v1:
time: 505 us; the launch traced here: 504 us
  waiting for transfers between devices  391 us (77%)
  starting transfers between devices  64.9 us (13%)
  local copies, waits for them, and re-layouts  34.1 us (7%)
  matrix products  11.5 us (2%)
    all_to_all x1, waiting for transfers between devices, track_series_all_up(): block_last = lax.all_to_all(finding, axis, concat_axis=0, split_axis=0)  200 us
    ppermute x2, waiting for transfers between devices, swapped(): return lax.ppermute(value, axis, pairs)  179 us
    all_to_all x1, starting transfers between devices, track_series_all_up(): block_last = lax.all_to_all(finding, axis, concat_axis=0, split_axis=0)  20.9 us
    ppermute x2, starting transfers between devices, with_halo(): before = lax.ppermute(last, axis, up)  19.3 us
    ppermute x2, starting transfers between devices, swapped(): return lax.ppermute(value, axis, pairs)  15.9 us
  transfers between devices with their start and end apart: 8, of which 6 were waited for; matrix products, arithmetic and copies ran while one was open for 5% of the time, Pallas kernels for 0%

profile of v1, /device:TPU:1, one launch (start us, length us, event | category | flops | bytes accessed | tf_op | source)
XLA Modules:
  0.0 504.1 jit_solution(2632544550579318873)
XLA Ops:
  0.7 5.0 all-to-all-start.1
  5.8 8.2 %all-to-all-done.1 = bf16[4,1,256,384]{3,2,1,0:T(8,128)(2,1)S(1)} async-done(((bf16[4,1,256,384]{3,2,1,0:T(8,128)(2,1)}), bf16[4,1,256,384]{3,2,1,0:T(8,128)(2,1)S(1)}, u32[]{:S(2)}, u32[]{:S(2)}) %all-to-all-start.1) | async-done | bytes 786464 | tf_op jit(solution)/shard_map/all_to_all | solution.py:79
  14.0 3.6 stack.2
  17.6 20.9 %all-to-all-start = ((bf16[64,12,3840]{2,1,0:T(8,128)(2,1)}), bf16[64,12,3840]{2,1,0:T(8,128)(2,1)}, u32[]{:S(2)}, u32[]{:S(2)}) async-start(bf16[64,12,3840]{2,1,0:T(8,128)(2,1)} %stack.2), calls=%async_computation | async-start | bytes 15728640 | tf_op jit(solution)/shard_map/all_to_all | solution.py:14
  38.6 7.9 %collective-permute-start = (bf16[256,768]{1,0:T(8,128)(2,1)S(1)}, bf16[256,768]{1,0:T(8,128)(2,1)S(1)}, u32[]{:S(2)}, u32[]{:S(2)}) collective-permute-start(bf16[256,768]{1,0:T(8,128)(2,1)S(1)} %slice_bitcast_fusion.9), channel_id=1, source_target_pairs={{0,4},{4,0},{1,5},{5,1},{2,6},{6,2},{3,7},{7,3},{8,12},{12,8},{9,1... | collective-permute-start | bytes 1179656 | tf_op jit(solution)/shard_map/ppermute | solution.py:31
  46.6 3.4 scatter_custom_fusion
  50.0 160.4 %collective-permute-done = bf16[256,768]{1,0:T(8,128)(2,1)S(1)} collective-permute-done((bf16[256,768]{1,0:T(8,128)(2,1)S(1)}, bf16[256,768]{1,0:T(8,128)(2,1)S(1)}, u32[]{:S(2)}, u32[]{:S(2)}) %collective-permute-start) | collective-permute-done | bytes 393248 | tf_op jit(solution)/shard_map/ppermute | solution.py:31
  210.6 2.7 gather_fusion
  215.3 200.5 %all-to-all-done = bf16[64,12,3840]{2,1,0:T(8,128)(2,1)} async-done(((bf16[64,12,3840]{2,1,0:T(8,128)(2,1)}), bf16[64,12,3840]{2,1,0:T(8,128)(2,1)}, u32[]{:S(2)}, u32[]{:S(2)}) %all-to-all-start) | async-done | bytes 5898272 | tf_op jit(solution)/shard_map/all_to_all | solution.py:14
  415.8 9.6 %reshape.24 = bf16[768,3840]{1,0:T(8,128)(2,1)} reshape(bf16[64,12,3840]{2,1,0:T(8,128)(2,1)} %all-to-all-done) | data formatting | bytes 11796480 | tf_op jit(solution)/shard_map/reshape | solution.py:15
  425.4 2.7 copy-done.1
  430.3 1.9 collective-permute-start.2
  432.3 3.6 copy.18
  435.9 3.6 collective-permute-start.1
  439.5 1.8 fusion.6
  441.4 2.7 gather_fusion.1
  444.2 8.0 %collective-permute-start.3 = (bf16[256,768]{0,1:T(8,128)(2,1)S(1)}, bf16[256,768]{0,1:T(8,128)(2,1)S(1)}, u32[]{:S(2)}, u32[]{:S(2)}) collective-permute-start(bf16[256,768]{0,1:T(8,128)(2,1)S(1)} %select_bitcast_fusion), channel_id=1, source_target_pairs={{0,4},{4,0},{1,5},{5,1},{2,6},{6,2},{3,7},{7,3},{8,12},{12,8},{9,1... | collective-permute-start | bytes 1179656 | tf_op jit(solution)/shard_map/ppermute | solution.py:31
  452.2 1.9 fusion.8
  454.1 1.9 fusion.10
  457.2 2.3 fusion.4
  460.4 18.2 %collective-permute-done.3 = bf16[256,768]{0,1:T(8,128)(2,1)S(1)} collective-permute-done((bf16[256,768]{0,1:T(8,128)(2,1)S(1)}, bf16[256,768]{0,1:T(8,128)(2,1)S(1)}, u32[]{:S(2)}, u32[]{:S(2)}) %collective-permute-start.3) | collective-permute-done | bytes 393248 | tf_op jit(solution)/shard_map/ppermute | solution.py:31
  479.6 15.7 %collective-permute-start.5 = (bf16[128,768]{1,0:T(8,128)(2,1)S(1)}, bf16[128,768]{1,0:T(8,128)(2,1)S(1)}, u32[]{:S(2)}, u32[]{:S(2)}) collective-permute-start(bf16[128,768]{1,0:T(8,128)(2,1)S(1)} %get-tuple-element.8), channel_id=1, source_target_pairs={{0,8},{8,16},{16,24},{24,32},{32,40},{40,48},{48,56},{56,64},{64,7... | collective-permute-start | bytes 589832 | tf_op jit(solution)/shard_map/ppermute | solution.py:41
  495.3 1.9 collective-permute-start.4
  498.5 3.8 collective-permute-done.4
  (63 shorter events, 11.0 us)
Async XLA Ops:
  0.6 5.0 copy-start.9
  0.6 5.1 %copy-start.11 = (bf16[12,768]{1,0:T(8,128)(2,1)S(1)}, bf16[12,768]{1,0:T(8,128)(2,1)}, u32[]{:S(2)}) copy-start(bf16[12,768]{1,0:T(8,128)(2,1)} %param.11) | copy-start | bytes 55300
  0.7 5.1 %copy-start.10 = (bf16[12,768]{1,0:T(8,128)(2,1)S(1)}, bf16[12,768]{1,0:T(8,128)(2,1)}, u32[]{:S(2)}) copy-start(bf16[12,768]{1,0:T(8,128)(2,1)} %param.12) | copy-start | bytes 55300
  0.7 13.3 %all-to-all-start.1 = ((bf16[4,1,256,384]{3,2,1,0:T(8,128)(2,1)}), bf16[4,1,256,384]{3,2,1,0:T(8,128)(2,1)S(1)}, u32[]{:S(2)}, u32[]{:S(2)}) async-start(bf16[4,1,256,384]{3,2,1,0:T(8,128)(2,1)} %param.9), calls=%async_computation.1 | async-start | bytes 1572864 | tf_op jit(solution)/shard_map/all_to_all | solution.py:79
  17.6 20.9 %copy-start.6 = (bf16[1,1,256,1536]{3,2,1,0:T(8,128)(2,1)S(1)}, bf16[1,1,256,1536]{3,2,1,0:T(8,128)(2,1)}, u32[]{:S(2)}) copy-start(bf16[1,1,256,1536]{3,2,1,0:T(8,128)(2,1)} %param.8) | copy-start | bytes 2359300
  17.6 28.9 %copy-start.12 = (s32[768]{0:T(1024)S(1)}, s32[768]{0:T(1024)}, u32[]{:S(2)}) copy-start(s32[768]{0:T(1024)} %param.13) | copy-start | bytes 9220
  17.6 398.2 %all-to-all-start = ((bf16[64,12,3840]{2,1,0:T(8,128)(2,1)}), bf16[64,12,3840]{2,1,0:T(8,128)(2,1)}, u32[]{:S(2)}, u32[]{:S(2)}) async-start(bf16[64,12,3840]{2,1,0:T(8,128)(2,1)} %stack.2), calls=%async_computation | async-start | bytes 15728640 | tf_op jit(solution)/shard_map/all_to_all | solution.py:14
  38.6 171.8 %collective-permute-start = (bf16[256,768]{1,0:T(8,128)(2,1)S(1)}, bf16[256,768]{1,0:T(8,128)(2,1)S(1)}, u32[]{:S(2)}, u32[]{:S(2)}) collective-permute-start(bf16[256,768]{1,0:T(8,128)(2,1)S(1)} %slice_bitcast_fusion.9), channel_id=1, source_target_pairs={{0,4},{4,0},{1,5},{5,1},{2,6},{6,2},{3,7},{7,3},{8,12},{12,8},{9,1... | collective-permute-start | bytes 1179656 | tf_op jit(solution)/shard_map/ppermute | solution.py:31
  425.4 2.7 copy-start.1
  425.4 2.7 copy-start.5
  425.4 3.0 copy-start.7
  428.3 3.9 slice-start.2
  428.8 0.7 copy-start.2
  430.3 23.8 %collective-permute-start.2 = (bf16[128,768]{1,0:T(8,128)(2,1)}, bf16[128,768]{1,0:T(8,128)(2,1)}, u32[]{:S(2)}, u32[]{:S(2)}) collective-permute-start(bf16[128,768]{1,0:T(8,128)(2,1)} %get-tuple-element.10), channel_id=1, source_target_pairs={{8,0},{16,8},{24,16},{32,24},{40,32},{48,40},{56,48},{64,56},{72,6... | collective-permute-start | bytes 589832 | tf_op jit(solution)/shard_map/ppermute | solution.py:42
  435.9 20.2 %collective-permute-start.1 = (bf16[128,768]{1,0:T(8,128)(2,1)}, bf16[128,768]{1,0:T(8,128)(2,1)S(1)}, u32[]{:S(2)}, u32[]{:S(2)}) collective-permute-start(bf16[128,768]{1,0:T(8,128)(2,1)} %get-tuple-element.9), channel_id=1, source_target_pairs={{0,8},{8,16},{16,24},{24,32},{32,40},{40,48},{48,56},{56,64},{64,7... | collective-permute-start | bytes 589832 | tf_op jit(solution)/shard_map/ppermute | solution.py:41
  441.3 10.8 %copy-start.3 = (bf16[256,768]{1,0:T(8,128)(2,1)S(1)}, bf16[256,768]{1,0:T(8,128)(2,1)}, u32[]{:S(2)}) copy-start(bf16[256,768]{1,0:T(8,128)(2,1)} %copy-done.2) | copy-start | bytes 1179652
  444.2 34.4 %collective-permute-start.3 = (bf16[256,768]{0,1:T(8,128)(2,1)S(1)}, bf16[256,768]{0,1:T(8,128)(2,1)S(1)}, u32[]{:S(2)}, u32[]{:S(2)}) collective-permute-start(bf16[256,768]{0,1:T(8,128)(2,1)S(1)} %select_bitcast_fusion), channel_id=1, source_target_pairs={{0,4},{4,0},{1,5},{5,1},{2,6},{6,2},{3,7},{7,3},{8,12},{12,8},{9,1... | collective-permute-start | bytes 1179656 | tf_op jit(solution)/shard_map/ppermute | solution.py:31
  452.2 3.9 copy-start
  456.0 1.1 copy-start.8
  456.1 22.7 %slice-start = ((s8[5898240]{0:T(1024)(128)(4,1)}), s8[4194304]{0:T(1024)(128)(4,1)S(1)}, s32[]{:S(2)}) async-start(s8[5898240]{0:T(1024)(128)(4,1)} %bitcast.61), calls=%async_computation.2 | async-start | bytes 8388608
  457.2 21.6 %slice-start.1 = ((s8[5898240]{0:T(1024)(128)(4,1)}), s8[1703936]{0:T(1024)(128)(4,1)S(1)}, s32[]{:S(2)}) async-start(s8[5898240]{0:T(1024)(128)(4,1)} %bitcast.61), calls=%async_computation.3 | async-start | bytes 3407872
  459.4 19.1 %copy-start.4 = (bf16[1,1,256,4,384]{2,4,3,1,0:T(8,128)(2,1)S(1)}, bf16[1,1,256,4,384]{2,4,3,1,0:T(8,128)(2,1)}, u32[]{:S(2)}) copy-start(bf16[1,1,256,4,384]{2,4,3,1,0:T(8,128)(2,1)} %copy.22) | copy-start | bytes 2359300
  479.6 18.3 %collective-permute-start.5 = (bf16[128,768]{1,0:T(8,128)(2,1)S(1)}, bf16[128,768]{1,0:T(8,128)(2,1)S(1)}, u32[]{:S(2)}, u32[]{:S(2)}) collective-permute-start(bf16[128,768]{1,0:T(8,128)(2,1)S(1)} %get-tuple-element.8), channel_id=1, source_target_pairs={{0,8},{8,16},{16,24},{24,32},{32,40},{40,48},{48,56},{56,64},{64,7... | collective-permute-start | bytes 589832 | tf_op jit(solution)/shard_map/ppermute | solution.py:41
  495.3 7.0 %collective-permute-start.4 = (bf16[128,768]{1,0:T(8,128)(2,1)S(1)}, bf16[128,768]{1,0:T(8,128)(2,1)S(1)}, u32[]{:S(2)}, u32[]{:S(2)}) collective-permute-start(bf16[128,768]{1,0:T(8,128)(2,1)S(1)} %get-tuple-element.7), channel_id=1, source_target_pairs={{8,0},{16,8},{24,16},{32,24},{40,32},{48,40},{56,48},{64,56},{72,6... | collective-permute-start | bytes 589832 | tf_op jit(solution)/shard_map/ppermute | solution.py:42
